TPU v7x, 32 devices: a whole 2x2x4 slice. The times are simulated.
32 devices in a mesh: dp: 4 (over y, core), expert: 8 (over z, x).
Axes of the slice: x: 2, y: 2, z: 4, core: 2. Of those that a mesh axis runs over, the one named last changes fastest.
Arguments:
- text: bfloat16 [4096, 5120], P(('dp', 'expert')), may hold values from -6 to 6
- patches: bfloat16 [4, 24, 24, 1408], P('dp', None, None, 'expert'), may hold values from -6 to 6
- vis_start: int32 [4], P('dp'), may hold values from 0 to 880
- fc1: bfloat16 [4, 1408, 4096], P(None, 'expert', 'dp'), may hold values from -0.078125 to 0.078125
- fc2: bfloat16 [4096, 4096], P('expert', 'dp'), may hold values from -0.09375 to 0.09375
- proj: bfloat16 [4096, 5120], P('expert', 'dp'), may hold values from -0.09375 to 0.09375
- norm_gain: bfloat16 [5120], replicated, may hold values from 0.099609375 to 1.8984375
- router: bfloat16 [5120, 8], replicated, may hold values from -0.078125 to 0.078125
- routes: int32 [4096, 1], P(('dp', 'expert')), may hold values from 0 to 7; in each aligned block of 128 rows (0 to 127, 128 to 255, ...) at most 20 rows name the same one
- gate_w: bfloat16 [8, 5120, 4096], P('expert', None, 'dp'), may hold values from -0.15625 to 0.15625
- up_w: bfloat16 [8, 5120, 4096], P('expert', None, 'dp'), may hold values from -0.15625 to 0.15625
- down_w: bfloat16 [8, 4096, 5120], P('expert', 'dp'), may hold values from -0.09375 to 0.09375
Outputs:
- layer_out: bfloat16 [4096, 5120], P(('dp', 'expert'))
Inputs may be any that keep to these rules, and one draw needn't show every extreme that they name: `routes`: among the 128 positions of one device each expert is named at most 20 times. The image of sequence n fills the 144 positions from vis_start[n] on.
All inputs are finite; a program needn't handle non-finite values.
Results may differ from a plain program's by a relative error of at most 0.024.
Values may be sent and summed in bfloat16 or wider, within the bound.
A program may use at most 128 MiB of HBM per device.

v0:
```python
import functools

import jax
import jax.numpy as jnp
from jax import lax
from jax.experimental import pallas as pl
from jax.experimental.pallas import tpu as pltpu
from jax.sharding import PartitionSpec as P

EPSILON = 1e-05
MESH = pl.DeviceIdType.MESH


def send(src, dst, send_sem, recv_sem, d, e):
    return pltpu.make_async_remote_copy(
        src_ref=src,
        dst_ref=dst,
        send_sem=send_sem,
        recv_sem=recv_sem,
        device_id={"dp": d, "expert": e},
        device_id_type=MESH,
    )


def greet(d, e):
    pl.semaphore_signal(
        pltpu.get_barrier_semaphore(),
        inc=1,
        device_id={"dp": d, "expert": e},
        device_id_type=MESH,
    )


def turn(index, step):
    bit = 1
    while bit <= step:
        if step & bit:
            index = index + bit - 2 * bit * lax.rem(index // bit, 2)
        bit *= 2
    return index


def far_first(count):
    order, high = [], count // 2
    while high:
        order += range(high, 2 * high)
        high //= 2
    return order + [0]


def mixed(count):
    near, far = list(range(count // 2)), list(range(count // 2, count))
    order = near[:2]
    for i, step in enumerate(far):
        order.append(step)
        if i > 0 and i + 1 < len(near):
            order.append(near[i + 1])
    return order


def keep(src, dst, bounce, sem):
    first = pltpu.make_async_copy(src, bounce, sem)
    first.start()
    first.wait()
    second = pltpu.make_async_copy(bounce, dst, sem)
    second.start()
    second.wait()


def call(kernel, x, out_shape, scratch, sem_counts, collective_id, space=pl.ANY):
    return pl.pallas_call(
        kernel,
        out_shape=jax.ShapeDtypeStruct(out_shape, x.dtype),
        in_specs=[pl.BlockSpec(memory_space=space)],
        out_specs=pl.BlockSpec(memory_space=space),
        scratch_shapes=[pltpu.VMEM(shape, x.dtype) for shape in scratch]
        + [pltpu.SemaphoreType.DMA]
        + [pltpu.SemaphoreType.DMA((count,)) for count in sem_counts],
        compiler_params=pltpu.CompilerParams(
            collective_id=collective_id, has_side_effects=True
        ),
    )(x)


def cross_kernel(n_dp, x, out, landed, paired, summed, loc, s1, r1, s2, r2, s3, r3):
    d, e = lax.axis_index("dp"), lax.axis_index("expert")
    side, place = lax.rem(e, 2), e // 2
    width = out.shape[2]
    mine = pl.ds(pl.multiple_of(side * width, 128), width)
    theirs = pl.ds(pl.multiple_of((1 - side) * width, 128), width)
    mate = place * 2 + 1 - side
    for j in range(1, n_dp):
        greet(lax.rem(d + j, n_dp), e)
        greet(d, lax.rem(place + j, n_dp) * 2 + side)
    greet(d, mate)
    pl.semaphore_wait(pltpu.get_barrier_semaphore(), 2 * n_dp - 1)
    first, second = [], []
    for j in range(1, n_dp):
        to_d = lax.rem(d + j, n_dp)
        first.append(send(x.at[to_d], landed.at[j], s1.at[j], r1.at[j], to_d, e))
        first[-1].start()

    def source(j):
        return x.at[d] if j == 0 else landed.at[j]

    def third(j):
        owner = lax.rem(d + n_dp - j, n_dp)
        moved = send(
            summed.at[j], out.at[place], s3.at[j], r3.at[place], d, owner * 2 + side
        )
        return owner != place, moved

    def add(j):
        second[j].wait_recv()
        own = x[d, :, mine] if j == 0 else landed[j, :, mine]
        total = own.astype(jnp.float32) + paired[j].astype(jnp.float32)
        summed[j] = total.astype(summed.dtype)
        away, _ = third(j)

        @pl.when(jnp.logical_not(away))
        def _():
            out[place] = total.astype(out.dtype)

    for j in range(n_dp):
        if j > 0:
            first[j - 1].wait_recv()
        second.append(send(source(j).at[:, theirs], paired.at[j], s2.at[j], r2.at[j], d, mate))
        second[j].start()
        if j > 0:
            add(j - 1)
        if j > 1:
            away, moved = third(j - 2)
            pl.when(away)(moved.start)
    add(n_dp - 1)
    for j in (n_dp - 2, n_dp - 1):
        away, moved = third(j)
        pl.when(away)(moved.start)
    for other in range(n_dp):
        @pl.when(other != place)
        def _():
            send(
                summed.at[0], out.at[other], s3.at[0], r3.at[other], d, other * 2 + side
            ).wait_recv()
    for j in range(n_dp):
        away, moved = third(j)
        pl.when(away)(moved.wait_send)
    for moved in first + second:
        moved.wait_send()


def cross(part, n_dp, collective_id):
    x = part.astype(jnp.bfloat16).reshape(n_dp, part.shape[0] // n_dp, part.shape[1])
    width = x.shape[2] // 2
    spare = -width % 128
    if spare:
        x = x.reshape(n_dp, x.shape[1], 2, width)
        x = jnp.pad(x, ((0, 0), (0, 0), (0, 0), (0, spare)))
        x = x.reshape(n_dp, x.shape[1], 2 * (width + spare))
    half = (n_dp, x.shape[1], width + spare)
    out = call(
        functools.partial(cross_kernel, n_dp),
        x, half, (x.shape, half, half), (n_dp,) * 6, collective_id, pltpu.VMEM,
    )
    return out[:, :, :width] if spare else out


def gather_expert_kernel(n_exp, x, out, bounce, loc, s_sem, r_sem, sp_sem, rp_sem):
    d, e = lax.axis_index("dp"), lax.axis_index("expert")
    side, place = lax.rem(e, 2), e // 2
    half = n_exp // 2
    mate = place * 2 + 1 - side
    greet(d, mate)
    for i in range(1, half):
        greet(d, lax.rem(place + i, half) * 2 + side)
    pl.semaphore_wait(pltpu.get_barrier_semaphore(), half)
    near = [send(x, out.at[e], sp_sem.at[0], rp_sem.at[0], d, mate)]
    near[0].start()
    far = []
    for i in range(1, half):
        to_e = lax.rem(place + i, half) * 2 + side
        far.append(send(x, out.at[e], s_sem.at[i], r_sem.at[i], d, to_e))
        far[-1].start()
    keep(x, out.at[e], bounce, loc)
    for i in range(1, half):
        far[i - 1].wait_recv()
        block = out.at[lax.rem(place + half - i, half) * 2 + side]
        near.append(send(block, block, sp_sem.at[i], rp_sem.at[i], d, mate))
        near[i].start()
    for moved in near:
        moved.wait()
    for moved in far:
        moved.wait_send()


def gather_expert(x, n_exp, collective_id):
    return call(
        functools.partial(gather_expert_kernel, n_exp),
        x, (n_exp,) + x.shape, (x.shape,), (n_exp // 2,) * 4, collective_id, pltpu.VMEM,
    )


def gather_dp_kernel(n_dp, x, out, bounce, loc, s_sem, r_sem, sp_sem, rp_sem):
    d, e = lax.axis_index("dp"), lax.axis_index("expert")
    ny = n_dp // 2
    y, c = d // 2, lax.rem(d, 2)
    partner = y * 2 + 1 - c
    greet(partner, e)
    for i in range(1, ny):
        greet(lax.rem(y + i, ny) * 2 + c, e)
    pl.semaphore_wait(pltpu.get_barrier_semaphore(), ny)
    far = [
        send(x, out.at[d], s_sem.at[i], r_sem.at[i], lax.rem(y + i, ny) * 2 + c, e)
        for i in range(1, ny)
    ]
    for moved in far:
        moved.start()
    near = [send(x, out.at[d], sp_sem.at[0], rp_sem.at[0], partner, e)]
    near[0].start()
    keep(x, out.at[d], bounce, loc)
    for i in range(1, ny):
        far[i - 1].wait_recv()
        slot = lax.rem(y + ny - i, ny) * 2 + c
        near.append(send(out.at[slot], out.at[slot], sp_sem.at[i], rp_sem.at[i], partner, e))
        near[i].start()
    for moved in near:
        moved.wait()
    for moved in far:
        moved.wait_send()


def gather_dp(x, n_dp, collective_id):
    ny = n_dp // 2
    return call(
        functools.partial(gather_dp_kernel, n_dp),
        x, (n_dp,) + x.shape, (x.shape,), (ny, ny, ny, ny), collective_id, pltpu.VMEM,
    )


def dispatch_kernel(n_dp, n_exp, x, out, bounce, loc, s1, r1, sy, ry, sp, rp):
    d, e = lax.axis_index("dp"), lax.axis_index("expert")
    ny = n_dp // 2
    y, c = d // 2, lax.rem(d, 2)
    partner = y * 2 + 1 - c
    greet(partner, e)
    for i in range(1, n_exp):
        greet(d, turn(e, i))
    for j in range(1, ny):
        greet(lax.rem(y + j, ny) * 2 + c, e)
    pl.semaphore_wait(pltpu.get_barrier_semaphore(), n_exp + ny - 1)
    first, far, near = {}, {}, []
    for i in far_first(n_exp):
        if i > 0:
            to_e = turn(e, i)
            first[i] = send(x.at[to_e], out.at[d, e], s1.at[i], r1.at[i], d, to_e)
            first[i].start()

    def spread(i):
        slot = turn(e, i)
        if i > 0:
            first[i].wait_recv()
        block = x.at[e] if i == 0 else out.at[d, slot]
        for j in range(1, ny):
            index = i * ny + j
            moved = send(
                block, out.at[d, slot], sy.at[index], ry.at[index], lax.rem(y + j, ny) * 2 + c, e
            )
            moved.start()
            far[index] = moved
        moved = send(block, out.at[d, slot], sp.at[i * ny], rp.at[i * ny], partner, e)
        moved.start()
        near.append(moved)

    def relay(i):
        slot = turn(e, i)
        for j in range(1, ny):
            index = i * ny + j
            far[index].wait_recv()
            block = out.at[lax.rem(y + ny - j, ny) * 2 + c, slot]
            moved = send(block, block, sp.at[index], rp.at[index], partner, e)
            moved.start()
            near.append(moved)

    order = mixed(n_exp)
    for at, i in enumerate(order):
        spread(i)
        if i == 0:
            keep(x.at[e], out.at[d, e], bounce, loc)
        if at > 1:
            relay(order[at - 2])
    relay(order[-2])
    relay(order[-1])
    for moved in near:
        moved.wait()
    for moved in list(first.values()) + list(far.values()):
        moved.wait_send()


def dispatch(x, n_dp, n_exp, collective_id):
    count = n_dp // 2 * n_exp
    return call(
        functools.partial(dispatch_kernel, n_dp, n_exp),
        x, (n_dp,) + x.shape, (x.shape[1:],), (n_exp, n_exp) + (count,) * 4, collective_id,
    )


def swap_kernel(n_dp, x, out, bounce, loc, s_sem, r_sem):
    d, e = lax.axis_index("dp"), lax.axis_index("expert")
    ny = n_dp // 2
    y, c = d // 2, lax.rem(d, 2)
    partner = y * 2 + 1 - c
    greet(partner, e)
    pl.semaphore_wait(pltpu.get_barrier_semaphore(), 1)
    copies = [
        send(x.at[i, 1 - c], out.at[i], s_sem.at[i], r_sem.at[i], partner, e)
        for i in range(ny)
    ]
    for moved in copies:
        moved.start()
    for moved in copies:
        moved.wait()


def swap(x, n_dp, collective_id):
    ny = n_dp // 2
    return call(
        functools.partial(swap_kernel, n_dp),
        x, (ny,) + x.shape[2:], ((16, 128),), (ny, ny), collective_id,
    )


def home_kernel(n_dp, n_exp, x, out, landed, summed, loc, s1, r1, s2, r2):
    d, e = lax.axis_index("dp"), lax.axis_index("expert")
    ny = n_dp // 2
    y, c = d // 2, lax.rem(d, 2)
    for i in range(1, n_exp):
        greet(d, turn(e, i))
    for j in range(1, ny):
        greet(lax.rem(y + j, ny) * 2 + c, e)
    pl.semaphore_wait(pltpu.get_barrier_semaphore(), n_exp + ny - 2)
    columns = [turn(e, i) for i in far_first(n_exp)]
    first, second = [], []
    for i, column in enumerate(columns):
        for j in range(1, ny):
            to_y, index = lax.rem(y + j, ny), i * ny + j
            first.append(
                send(
                    x.at[to_y, column], landed.at[j, i],
                    s1.at[index], r1.at[index], to_y * 2 + c, e,
                )
            )
            first[-1].start()
    for i, column in enumerate(columns):
        total = x[y, column].astype(jnp.float32)
        for j in range(1, ny):
            first[i * (ny - 1) + j - 1].wait_recv()
            total = total + landed[j, i].astype(jnp.float32)
        if i < n_exp - 1:
            summed[i] = total.astype(summed.dtype)
            second.append(send(summed.at[i], out.at[e], s2.at[i], r2.at[i], d, column))
        else:
            out[e] = total.astype(out.dtype)
        if i > 0:
            second[i - 1].start()
    for moved in second:
        moved.wait()
    for moved in first:
        moved.wait_send()


def send_home(x, n_dp, n_exp, collective_id):
    ny = n_dp // 2
    return call(
        functools.partial(home_kernel, n_dp, n_exp),
        x, x.shape[1:], (x.shape, x.shape[1:]),
        (ny * n_exp, ny * n_exp, n_exp, n_exp), collective_id, pltpu.VMEM,
    )


def add_blocks(blocks):
    return jnp.sum(blocks.astype(jnp.float32), axis=0)


def on_device(
    text, patches, vis_start, fc1, fc2, proj, norm_gain, router, routes, gate_w, up_w, down_w
):
    expert_count = lax.axis_size("expert")
    my_column = lax.axis_index("expert")
    row_count = text.shape[0]
    feature = text.shape[1]
    grid_size = patches.shape[1]
    half_grid = grid_size // 2
    local_channels = patches.shape[3]
    vis_count = half_grid * half_grid
    shuffled = patches.reshape(half_grid, 2, half_grid, 2, local_channels)
    shuffled = shuffled.transpose(0, 2, 1, 3, 4).reshape(vis_count, 4 * local_channels)
    n_dp = lax.axis_size("dp")
    shuffled = gather_dp(shuffled, n_dp, 0).reshape(n_dp * vis_count, 4 * local_channels)
    weights = fc1.reshape(4 * local_channels, fc1.shape[2])
    pre_part = jnp.dot(shuffled, weights, preferred_element_type=jnp.float32)
    pre_act = add_blocks(cross(pre_part, n_dp, 1))
    activated = jax.nn.gelu(pre_act, approximate=False).astype(jnp.bfloat16)
    activated = gather_dp(activated, n_dp, 2).reshape(n_dp * vis_count, fc2.shape[0])
    middle_part = jnp.dot(activated, fc2, preferred_element_type=jnp.float32)
    middle_pre = add_blocks(cross(middle_part, n_dp, 3))
    middle = jax.nn.gelu(middle_pre, approximate=False).astype(jnp.bfloat16)
    middle = gather_dp(middle, n_dp, 4).reshape(n_dp * vis_count, proj.shape[0])
    visual_part = jnp.dot(middle, proj, preferred_element_type=jnp.float32)
    visual_own = add_blocks(
        cross(visual_part, n_dp, 5)
    ).astype(jnp.bfloat16)
    visual = gather_expert(visual_own, expert_count, 6)
    visual = visual.transpose(1, 0, 2).reshape(vis_count, feature)
    positions = my_column * row_count + jnp.arange(row_count, dtype=jnp.int32)
    offsets = positions - vis_start[0]
    in_image = (offsets >= 0) & (offsets < vis_count)
    picked = jnp.take(visual, jnp.clip(offsets, 0, vis_count - 1), axis=0)
    embedded = jnp.where(in_image[:, None], picked, text)
    embed_f32 = embedded.astype(jnp.float32)
    mean_square = jnp.mean(embed_f32 * embed_f32, axis=-1, keepdims=True)
    normed = (embed_f32 * lax.rsqrt(mean_square + EPSILON) * norm_gain.astype(jnp.float32)).astype(
        jnp.bfloat16
    )
    logits = jnp.dot(normed, router, preferred_element_type=jnp.float32)
    experts_all = router.shape[1]
    expert_id = routes[:, 0]
    one_hot = expert_id[:, None] == jnp.arange(experts_all, dtype=jnp.int32)[None, :]
    gate_score = jax.nn.sigmoid(jnp.sum(jnp.where(one_hot, logits, 0.0), axis=-1))
    routed_in = (normed.astype(jnp.float32) * gate_score[:, None]).astype(jnp.bfloat16)
    capacity = max(2, row_count * 5 // (4 * expert_count))
    row_ids = jnp.arange(row_count, dtype=jnp.int32)
    earlier_mask = (row_ids[None, :] < row_ids[:, None]).astype(jnp.bfloat16)
    earlier_counts = jnp.dot(
        earlier_mask, one_hot.astype(jnp.bfloat16), preferred_element_type=jnp.float32
    )
    slot_rank = jnp.sum(jnp.where(one_hot, earlier_counts, 0.0), axis=-1).astype(jnp.int32)
    slot_key = expert_id * capacity + slot_rank
    slot_ids = jnp.arange(experts_all * capacity, dtype=jnp.int32)
    dispatch_table = (slot_ids[:, None] == slot_key[None, :]).astype(jnp.bfloat16)
    outgoing = jnp.dot(dispatch_table, routed_in, preferred_element_type=jnp.float32).astype(
        jnp.bfloat16
    )
    outgoing = outgoing.reshape(experts_all, capacity, feature)
    gathered = dispatch(outgoing, n_dp, expert_count, 7)
    flat_rows = gathered.reshape(-1, feature)
    gate_act = jnp.dot(flat_rows, gate_w[0], preferred_element_type=jnp.float32)
    up_act = jnp.dot(flat_rows, up_w[0], preferred_element_type=jnp.float32)
    hidden = (jax.nn.silu(gate_act) * up_act).astype(jnp.bfloat16)
    partial_value = jnp.dot(hidden, down_w[0], preferred_element_type=jnp.float32)
    slots = experts_all * capacity
    partial_value = partial_value.astype(jnp.bfloat16).reshape(n_dp // 2, 2, slots, feature)
    core = lax.rem(lax.axis_index("dp"), 2)
    mine = lax.dynamic_index_in_dim(partial_value, core, axis=1, keepdims=False)
    pair = mine.astype(jnp.float32) + swap(partial_value, n_dp, 8).astype(jnp.float32)
    pair = pair.astype(jnp.bfloat16).reshape(n_dp // 2, experts_all, capacity, feature)
    expert_out = send_home(pair, n_dp, expert_count, 9)
    combined = lax.dot_general(
        dispatch_table,
        expert_out.reshape(experts_all * capacity, feature),
        (((0,), (0,)), ((), ())),
        preferred_element_type=jnp.float32,
    )
    return (embed_f32 + combined).astype(jnp.bfloat16)


def solution(mesh):
    return jax.shard_map(
        on_device,
        mesh=mesh,
        in_specs=(
            P(("dp", "expert"), None),
            P("dp", None, None, "expert"),
            P("dp"),
            P(None, "expert", "dp"),
            P("expert", "dp"),
            P("expert", "dp"),
            P(),
            P(),
            P(("dp", "expert"), None),
            P("expert", None, "dp"),
            P("expert", None, "dp"),
            P("expert", "dp", None),
        ),
        out_specs=P(("dp", "expert"), None),
        check_vma=False,
    )
```

profile of v0, /device:TPU:0, one launch (start us, length us, event | category | flops | bytes accessed | tf_op | source)
XLA Modules:
  0.0 381.2 jit_solution(5243178234597848096)
XLA Ops:
  5.9 12.1 %shard_map.118 = bf16[4,144,704]{2,1,0:T(8,128)(2,1)} custom-call(bf16[144,704]{1,0:T(8,128)(2,1)} %reshape.104.x), custom_call_target="tpu_custom_call" | custom-call | tf_op jit(solution)/shard_map/pallas_call | solution.py:71
  18.1 3.3 convolution_convert_fusion.3
  21.3 27.4 %shard_map.119 = bf16[4,144,512]{2,1,0:T(8,128)(2,1)} custom-call(bf16[4,144,1024]{2,1,0:T(8,128)(2,1)} %bitcast.58), custom_call_target="tpu_custom_call" | custom-call | tf_op jit(solution)/shard_map/pallas_call | solution.py:71
  51.2 15.0 %shard_map.120 = bf16[4,144,512]{2,1,0:T(8,128)(2,1)} custom-call(bf16[144,512]{1,0:T(8,128)(2,1)} %fusion.23.x), custom_call_target="tpu_custom_call" | custom-call | tf_op jit(solution)/shard_map/pallas_call | solution.py:71
  66.2 2.9 convolution_convert_fusion.2
  69.0 25.9 %shard_map.121 = bf16[4,144,512]{2,1,0:T(8,128)(2,1)} custom-call(bf16[4,144,1024]{2,1,0:T(8,128)(2,1)} %bitcast.59), custom_call_target="tpu_custom_call" | custom-call | tf_op jit(solution)/shard_map/pallas_call | solution.py:71
  97.4 14.8 %shard_map.122 = bf16[4,144,512]{2,1,0:T(8,128)(2,1)} custom-call(bf16[144,512]{1,0:T(8,128)(2,1)} %fusion.26.x), custom_call_target="tpu_custom_call" | custom-call | tf_op jit(solution)/shard_map/pallas_call | solution.py:71
  112.3 3.1 convolution_convert_fusion.1
  115.4 29.2 %shard_map.123 = bf16[4,144,640]{2,1,0:T(8,128)(2,1)} custom-call(bf16[4,144,1280]{2,1,0:T(8,128)(2,1)} %bitcast.57), custom_call_target="tpu_custom_call" | custom-call | tf_op jit(solution)/shard_map/pallas_call | solution.py:71
  144.7 1.9 reduce_sum.59.x
  146.6 31.2 %shard_map.124 = bf16[8,144,640]{2,1,0:T(8,128)(2,1)} custom-call(bf16[144,640]{1,0:T(8,128)(2,1)} %reduce_sum.59.x), custom_call_target="tpu_custom_call" | custom-call | tf_op jit(solution)/shard_map/pallas_call | solution.py:71
  180.7 2.1 fusion.11
  186.2 72.9 %shard_map.125 = bf16[4,8,20,5120]{3,2,1,0:T(8,128)(2,1)} custom-call(bf16[8,20,5120]{2,1,0:T(8,128)(2,1)} %reshape.113.x), custom_call_target="tpu_custom_call" | custom-call | tf_op jit(solution)/shard_map/pallas_call | solution.py:71
  259.1 8.7 %reshape.114 = bf16[640,5120]{1,0:T(8,128)(2,1)} reshape(bf16[4,8,20,5120]{3,2,1,0:T(8,128)(2,1)} %shard_map.125) | data formatting | bytes 13107200 | tf_op jit(solution)/shard_map/reshape | solution.py:444
  267.7 11.7 %fusion.2 = f32[640,1024]{1,0:T(8,128)S(1)} fusion(bf16[640,5120]{1,0:T(8,128)(2,1)} %reshape.114, bf16[1,5120,1024]{2,1,0:T(8,128)(2,1)} %param.22), kind=kOutput, calls=%fused_computation.3 | convolution fusion | flops 6710886400 | bytes 19660800 | tf_op jit(solution)/shard_map/dot_general | solution.py:446
  279.4 10.2 %multiply_convert_fusion = bf16[640,1024]{1,0:T(8,128)(2,1)S(1)} fusion(f32[640,1024]{1,0:T(8,128)S(1)} %fusion.2, bf16[640,5120]{1,0:T(8,128)(2,1)S(1)} %copy-done.2, bf16[1,5120,1024]{2,1,0:T(8,128)(2,1)} %param.21), kind=kOutput, calls=%fused_computation.19 | convolution fusion | flops 6714818560 | bytes 20971520 | tf_op jit(solution)/shard_map/dot_general | solution.py:445
  289.6 8.9 %fusion.6 = bf16[640,5120]{1,0:T(8,128)(2,1)} fusion(bf16[640,1024]{1,0:T(8,128)(2,1)S(1)} %multiply_convert_fusion, bf16[1,1024,5120]{2,1,0:T(8,128)(2,1)S(1)} %bitcast.65), kind=kOutput, calls=%fused_computation.7 | convolution fusion | flops 6714163200 | bytes 18350080 | tf_op jit(solution)/shard_map/dot_general | solution.py:448
  298.6 6.2 %shard_map.126 = bf16[2,160,5120]{2,1,0:T(8,128)(2,1)} custom-call(bf16[2,2,160,5120]{3,2,1,0:T(8,128)(2,1)} %bitcast.53), custom_call_target="tpu_custom_call" | custom-call | tf_op jit(solution)/shard_map/pallas_call | solution.py:71
  304.8 4.1 %fusion.9 = bf16[2,160,5120]{2,1,0:T(8,128)(2,1)S(1)} fusion(bf16[2,160,5120]{2,1,0:T(8,128)(2,1)} %shard_map.126, bf16[2,2,160,5120]{3,2,1,0:T(8,128)(2,1)} %bitcast.54, s32[]{:T(128)S(6)} %select_n.41), kind=kLoop, calls=%fused_computation.9 | loop fusion | flops 6553600 | bytes 9830404 | tf_op jit(solution)/shard_map/convert_element_type | solution.py:454
  308.9 3.4 copy.16
  312.3 2.7 copy.17.x
  315.1 61.4 %shard_map.127 = bf16[8,20,5120]{2,1,0:T(8,128)(2,1)} custom-call(bf16[2,8,20,5120]{3,2,1,0:T(8,128)(2,1)} %copy.17.x), custom_call_target="tpu_custom_call" | custom-call | tf_op jit(solution)/shard_map/pallas_call | solution.py:71
  376.4 1.8 reshape.117
  378.2 2.9 fusion.10
  (43 shorter events, 16.3 us)
Async XLA Ops:
  0.0 1.4 copy-start
  21.3 44.8 %copy-start.5 = (bf16[512,1024]{1,0:T(8,128)(2,1)S(1)}, bf16[512,1024]{1,0:T(8,128)(2,1)}, u32[]{:S(2)}) copy-start(bf16[512,1024]{1,0:T(8,128)(2,1)} %param.16) | copy-start | bytes 3145732
  69.0 43.2 %copy-start.4 = (bf16[512,1280]{1,0:T(8,128)(2,1)S(1)}, bf16[512,1280]{1,0:T(8,128)(2,1)}, u32[]{:S(2)}) copy-start(bf16[512,1280]{1,0:T(8,128)(2,1)} %param.17) | copy-start | bytes 3932164
  180.7 2.1 copy-start.6
  180.7 2.1 copy-start.7
  182.8 1.1 copy-start.3
  267.7 11.7 %copy-start.2 = (bf16[640,5120]{1,0:T(8,128)(2,1)S(1)}, bf16[640,5120]{1,0:T(8,128)(2,1)}, u32[]{:S(2)}) copy-start(bf16[640,5120]{1,0:T(8,128)(2,1)} %reshape.114) | copy-start | bytes 19660804
  267.7 21.9 %slice-start = ((s8[10485760]{0:T(1024)(128)(4,1)}), s8[4194304]{0:T(1024)(128)(4,1)S(1)}, s32[]{:S(2)}) async-start(s8[10485760]{0:T(1024)(128)(4,1)} %bitcast.64), calls=%async_computation | async-start | bytes 8388608
  267.7 21.9 %slice-start.1 = ((s8[10485760]{0:T(1024)(128)(4,1)}), s8[4194304]{0:T(1024)(128)(4,1)S(1)}, s32[]{:S(2)}) async-start(s8[10485760]{0:T(1024)(128)(4,1)} %bitcast.64), calls=%async_computation.1 | async-start | bytes 8388608
  279.4 10.2 %slice-start.2 = ((s8[10485760]{0:T(1024)(128)(4,1)}), s8[2097152]{0:T(1024)(128)(4,1)S(1)}, s32[]{:S(2)}) async-start(s8[10485760]{0:T(1024)(128)(4,1)} %bitcast.64), calls=%async_computation.2 | async-start | bytes 4194304
  376.4 4.8 %copy-start.1 = (bf16[4,176,1024]{2,1,0:T(8,128)(2,1)S(1)}, bf16[4,176,1024]{2,1,0:T(8,128)(2,1)}, u32[]{:S(2)}) copy-start(bf16[4,176,1024]{2,1,0:T(8,128)(2,1)} %param.15) | copy-start | bytes 4325380
where the time goes:
time: 382 us; the launch traced here: 381 us
  Pallas kernels  296 us (77%)
  matrix products  45.1 us (12%)
  local copies, waits for them, and re-layouts  24.3 us (6%)
  other arithmetic  14.5 us (4%)
    pallas_call x10, Pallas kernels, call(): pl.pallas_call(kernel, out_shape=jax.ShapeDtypeStruct(out_shape, x.dtype)...  296 us
    dot_general x1, matrix products, on_device(): up_act = jnp.dot(flat_rows, up_w[0], preferred_element_type=jnp.float32)  11.7 us
    dot_general x1, matrix products, on_device(): gate_act = jnp.dot(flat_rows, gate_w[0], preferred_element_type=jnp.float32)  10.2 us
    dot_general x1, matrix products, on_device(): jnp.dot(hidden, down_w[0], preferred_element_type=jnp.float32)  8.92 us
    reshape x1, local copies, waits for them, and re-layouts, on_device(): flat_rows = gathered.reshape(-1, feature)  8.66 us

commit v1 on v0

--- a/solution.py
+++ b/solution.py
@@ -427,6 +427,7 @@
     gate_score = jax.nn.sigmoid(jnp.sum(jnp.where(one_hot, logits, 0.0), axis=-1))
     routed_in = (normed.astype(jnp.float32) * gate_score[:, None]).astype(jnp.bfloat16)
     capacity = max(2, row_count * 5 // (4 * expert_count))
+    capacity += -capacity % 8
     row_ids = jnp.arange(row_count, dtype=jnp.int32)
     earlier_mask = (row_ids[None, :] < row_ids[:, None]).astype(jnp.bfloat16)
     earlier_counts = jnp.dot(

time: 382 us -> 372 us (0.974)
  local copies, waits for them, and re-layouts: 24.3 us -> 5.75 us
  matrix products: 45.1 us -> 50.4 us
    reshape x4 -> x0, local copies, waits for them, and re-layouts: 14.7 us -> none  [the longest x1 8.66 us: on_device(): flat_rows = gathered.reshape(-1, feature)]
where the time goes in v1:
time: 372 us
  Pallas kernels  297 us (80%)
  matrix products  50.4 us (14%)
  other arithmetic  17.2 us (5%)
  local copies, waits for them, and re-layouts  5.75 us (2%)
    pallas_call x10, Pallas kernels, call(): pl.pallas_call(kernel, out_shape=jax.ShapeDtypeStruct(out_shape, x.dtype)...  297 us
    dot_general x1, matrix products, on_device(): up_act = jnp.dot(flat_rows, up_w[0], preferred_element_type=jnp.float32)  12.3 us
    dot_general x1, matrix products, on_device(): gate_act = jnp.dot(flat_rows, gate_w[0], preferred_element_type=jnp.float32)  11.7 us
    dot_general x1, matrix products, on_device(): jnp.dot(hidden, down_w[0], preferred_element_type=jnp.float32)  10.4 us

profile of v1, /device:TPU:0, one launch (start us, length us, event | category | flops | bytes accessed | tf_op | source)
XLA Modules:
  0.0 371.6 jit_solution(9192122357532752482)
XLA Ops:
  5.9 12.1 %shard_map.118 = bf16[4,144,704]{2,1,0:T(8,128)(2,1)} custom-call(bf16[144,704]{1,0:T(8,128)(2,1)} %reshape.104.x), custom_call_target="tpu_custom_call" | custom-call | tf_op jit(solution)/shard_map/pallas_call | solution.py:71
  18.1 3.3 convolution_convert_fusion.3
  21.3 27.4 %shard_map.119 = bf16[4,144,512]{2,1,0:T(8,128)(2,1)} custom-call(bf16[4,144,1024]{2,1,0:T(8,128)(2,1)} %bitcast.65), custom_call_target="tpu_custom_call" | custom-call | tf_op jit(solution)/shard_map/pallas_call | solution.py:71
  49.9 1.3 fusion.23.x
  51.2 15.0 %shard_map.120 = bf16[4,144,512]{2,1,0:T(8,128)(2,1)} custom-call(bf16[144,512]{1,0:T(8,128)(2,1)} %fusion.23.x), custom_call_target="tpu_custom_call" | custom-call | tf_op jit(solution)/shard_map/pallas_call | solution.py:71
  66.2 2.9 convolution_convert_fusion.2
  69.0 25.9 %shard_map.121 = bf16[4,144,512]{2,1,0:T(8,128)(2,1)} custom-call(bf16[4,144,1024]{2,1,0:T(8,128)(2,1)} %bitcast.66), custom_call_target="tpu_custom_call" | custom-call | tf_op jit(solution)/shard_map/pallas_call | solution.py:71
  97.4 14.8 %shard_map.122 = bf16[4,144,512]{2,1,0:T(8,128)(2,1)} custom-call(bf16[144,512]{1,0:T(8,128)(2,1)} %fusion.26.x), custom_call_target="tpu_custom_call" | custom-call | tf_op jit(solution)/shard_map/pallas_call | solution.py:71
  112.3 3.1 convolution_convert_fusion.1
  115.4 29.2 %shard_map.123 = bf16[4,144,640]{2,1,0:T(8,128)(2,1)} custom-call(bf16[4,144,1280]{2,1,0:T(8,128)(2,1)} %bitcast.64), custom_call_target="tpu_custom_call" | custom-call | tf_op jit(solution)/shard_map/pallas_call | solution.py:71
  144.7 1.9 reduce_sum.59.x
  146.6 31.2 %shard_map.124 = bf16[8,144,640]{2,1,0:T(8,128)(2,1)} custom-call(bf16[144,640]{1,0:T(8,128)(2,1)} %reduce_sum.59.x), custom_call_target="tpu_custom_call" | custom-call | tf_op jit(solution)/shard_map/pallas_call | solution.py:71
  177.8 1.6 copy.16
  179.4 1.3 gather_fusion
  180.7 2.1 fusion.11
  183.4 2.2 convolution_convert_fusion
  185.5 72.9 %shard_map.125 = bf16[4,8,24,5120]{3,2,1,0:T(8,128)(2,1)} custom-call(bf16[8,24,5120]{2,1,0:T(8,128)(2,1)} %bitcast.63), custom_call_target="tpu_custom_call" | custom-call | tf_op jit(solution)/shard_map/pallas_call | solution.py:71
  258.5 12.3 %fusion.2 = f32[768,1024]{1,0:T(8,128)S(1)} fusion(bf16[768,5120]{1,0:T(8,128)(2,1)} %bitcast.59, bf16[1,5120,1024]{2,1,0:T(8,128)(2,1)} %param.22), kind=kOutput, calls=%fused_computation.3 | convolution fusion | flops 8053063680 | bytes 21495808 | tf_op jit(solution)/shard_map/dot_general | solution.py:447
  270.8 11.7 %multiply_convert_fusion = bf16[768,1024]{1,0:T(8,128)(2,1)S(1)} fusion(f32[768,1024]{1,0:T(8,128)S(1)} %fusion.2, bf16[768,5120]{1,0:T(8,128)(2,1)S(1)} %bitcast.60, bf16[1,5120,1024]{2,1,0:T(8,128)(2,1)} %param.21), kind=kOutput, calls=%fused_computation.15 | convolution fusion | flops 8057782272 | bytes 23068672 | tf_op jit(solution)/shard_map/dot_general | solution.py:446
  282.5 10.4 %fusion.6 = bf16[768,5120]{1,0:T(8,128)(2,1)} fusion(bf16[768,1024]{1,0:T(8,128)(2,1)S(1)} %multiply_convert_fusion, bf16[1,1024,5120]{2,1,0:T(8,128)(2,1)S(1)} %bitcast.72), kind=kOutput, calls=%fused_computation.7 | convolution fusion | flops 8056995840 | bytes 19922944 | tf_op jit(solution)/shard_map/dot_general | solution.py:449
  293.0 7.2 %shard_map.126 = bf16[2,192,5120]{2,1,0:T(8,128)(2,1)} custom-call(bf16[2,2,192,5120]{3,2,1,0:T(8,128)(2,1)} %bitcast.56), custom_call_target="tpu_custom_call" | custom-call | tf_op jit(solution)/shard_map/pallas_call | solution.py:71
  300.1 6.8 %fusion.9 = bf16[2,192,5120]{2,1,0:T(8,128)(2,1)} fusion(bf16[2,192,5120]{2,1,0:T(8,128)(2,1)} %shard_map.126, bf16[2,2,192,5120]{3,2,1,0:T(8,128)(2,1)} %bitcast.57, s32[]{:T(128)S(6)} %select_n.41), kind=kLoop, calls=%fused_computation.9 | loop fusion | flops 7864320 | bytes 11796484 | tf_op jit(solution)/shard_map/convert_element_type | solution.py:455
  306.9 61.5 %shard_map.127 = bf16[8,24,5120]{2,1,0:T(8,128)(2,1)} custom-call(bf16[2,8,24,5120]{3,2,1,0:T(8,128)(2,1)} %bitcast.58), custom_call_target="tpu_custom_call" | custom-call | tf_op jit(solution)/shard_map/pallas_call | solution.py:71
  368.4 3.2 fusion.10
  (36 shorter events, 9.4 us)
Async XLA Ops:
  0.0 1.4 copy-start
  21.3 44.8 %copy-start.4 = (bf16[512,1024]{1,0:T(8,128)(2,1)S(1)}, bf16[512,1024]{1,0:T(8,128)(2,1)}, u32[]{:S(2)}) copy-start(bf16[512,1024]{1,0:T(8,128)(2,1)} %param.16) | copy-start | bytes 3145732
  69.0 43.2 %copy-start.3 = (bf16[512,1280]{1,0:T(8,128)(2,1)S(1)}, bf16[512,1280]{1,0:T(8,128)(2,1)}, u32[]{:S(2)}) copy-start(bf16[512,1280]{1,0:T(8,128)(2,1)} %param.17) | copy-start | bytes 3932164
  180.7 2.1 copy-start.5
  180.7 2.1 copy-start.6
  258.4 12.4 %copy-start.2 = (bf16[4,8,24,5120]{3,2,1,0:T(8,128)(2,1)S(1)}, bf16[4,8,24,5120]{3,2,1,0:T(8,128)(2,1)}, u32[]{:S(2)}) copy-start(bf16[4,8,24,5120]{3,2,1,0:T(8,128)(2,1)} %shard_map.125) | copy-start | bytes 23592964
  258.4 24.1 %slice-start = ((s8[10485760]{0:T(1024)(128)(4,1)}), s8[4194304]{0:T(1024)(128)(4,1)S(1)}, s32[]{:S(2)}) async-start(s8[10485760]{0:T(1024)(128)(4,1)} %bitcast.71), calls=%async_computation | async-start | bytes 8388608
  258.5 24.1 %slice-start.1 = ((s8[10485760]{0:T(1024)(128)(4,1)}), s8[4194304]{0:T(1024)(128)(4,1)S(1)}, s32[]{:S(2)}) async-start(s8[10485760]{0:T(1024)(128)(4,1)} %bitcast.71), calls=%async_computation.1 | async-start | bytes 8388608
  270.8 11.7 %slice-start.2 = ((s8[10485760]{0:T(1024)(128)(4,1)}), s8[2097152]{0:T(1024)(128)(4,1)S(1)}, s32[]{:S(2)}) async-start(s8[10485760]{0:T(1024)(128)(4,1)} %bitcast.71), calls=%async_computation.2 | async-start | bytes 4194304
  306.9 64.6 %copy-start.1 = (bf16[4,176,1024]{2,1,0:T(8,128)(2,1)S(1)}, bf16[4,176,1024]{2,1,0:T(8,128)(2,1)}, u32[]{:S(2)}) copy-start(bf16[4,176,1024]{2,1,0:T(8,128)(2,1)} %param.15) | copy-start | bytes 4325380
